TPU v7x, 32 devices: a whole 2x2x4 slice. The times are simulated.
32 devices in a mesh: row: 4 (over y, core), col: 8 (over z, x).
Axes of the slice: x: 2, y: 2, z: 4, core: 2. Of those that a mesh axis runs over, the one named last changes fastest.
Arguments:
- factor: float32 [6, 2048, 6, 2048], P(None, 'row', None, 'col'), may hold values from -0.0625 to 0.0625
- diag_inv: float32 [6, 2048, 2048], P(None, None, 'row'), may hold values from -2 to 2, as said below
- structure: int32 [6, 6, 16], P(None, None, 'row'), may hold values 0 or 1
- parent: int32 [6], replicated, may hold values from 1 to 6, as said below
- post: float32 [6, 2048, 64], P(None, 'row', 'col'), may hold values from -6 to 6
Outputs:
- mean_x: float32 [6, 2048, 64], P(None, 'row', 'col')
- variance: float32 [6, 2048], P(None, 'row')
Inputs may be any that keep to these rules, and one draw needn't show every extreme that they name: parent[s] > s for s < 5, and parent[5] = 6; every supernode has at most 2 ancestors, and some supernode has exactly that many. The diagonal of each diag_inv[s] lies in 0.5 to 2.
All inputs are finite; a program needn't handle non-finite values. No bound on the sum of `structure` on one device may be relied on, other than what follows from the above.
Results may differ from a plain program's by a relative error of at most 0.00014.
Values sent between devices are 32-bit elements; how exact they have to be, the bound alone decides.
A program may use at most 192 MiB of HBM per device.

v0:
```python
import jax
import jax.numpy as jnp
from jax import lax
from jax.sharding import PartitionSpec as P

LEVELS = 3


HIGHEST = lax.Precision.HIGHEST


def contract(selected, panel_piece):
    return jnp.einsum("tiw,tin->wn", panel_piece, selected, precision=HIGHEST)


def body(factor, diag_inv, structure, parent, post):
    super_count = factor.shape[0]
    row_width = factor.shape[1]
    col_width = factor.shape[3]
    full_width = diag_inv.shape[1]
    rhs_width = post.shape[2]
    row_at = lax.axis_index("row")
    col_at = lax.axis_index("col")
    extended = jnp.concatenate([parent, jnp.full((1,), super_count, jnp.int32)])
    slot_ids = jnp.arange(super_count + 1, dtype=jnp.int32)
    targets = jnp.arange(super_count, dtype=jnp.int32)
    ancestor_hops = []
    current = parent
    for hop_index in range(super_count - 1):
        ancestor_hops.append(current)
        onehot = (current[:, None] == slot_ids[None, :]).astype(jnp.int32)
        current = jnp.sum(onehot * extended[None, :], axis=1)
    ancestry = jnp.zeros((super_count, super_count), jnp.float32)
    for hop_targets in ancestor_hops:
        ancestry = ancestry + (hop_targets[:, None] == targets[None, :]).astype(jnp.float32)
    block_rows = row_width // structure.shape[2]
    row_mask = jnp.repeat(structure.astype(jnp.float32), block_rows, axis=2) * ancestry[:, :, None]
    masked = factor * jnp.transpose(row_mask, (1, 2, 0))[:, :, :, None]
    rows_full = jnp.arange(full_width, dtype=jnp.int32)
    own_cols = row_at * row_width + jnp.arange(row_width, dtype=jnp.int32)
    lower_inv = jnp.where((rows_full[:, None] >= own_cols[None, :])[None, :, :], diag_inv, 0.0)
    unit_cols = col_at * col_width + jnp.arange(col_width, dtype=jnp.int32)
    unit_block = (rows_full[:, None] == unit_cols[None, :]).astype(jnp.float32)
    gathered = lax.all_gather(post, "row", axis=1, tiled=True)
    total_cols = super_count * col_width + rhs_width
    solution = jnp.zeros((super_count, row_width, total_cols), jnp.float32)
    for current_sup in range(super_count - 1, -1, -1):
        later_cols = (current_sup + 1) * col_width
        if current_sup == super_count - 1:
            summed = jnp.zeros((full_width, rhs_width), jnp.float32)
        else:
            picks = []
            chosen_rows = []
            for slot_index in range(LEVELS - 1):
                target = ancestor_hops[slot_index][current_sup]
                is_valid = (target < super_count).astype(jnp.float32)
                clamped = jnp.minimum(target, super_count - 1)
                picks.append(
                    lax.dynamic_index_in_dim(
                        masked[:, :, current_sup, :], clamped, 0, keepdims=False
                    )
                    * is_valid
                )
                chosen_rows.append(
                    lax.dynamic_index_in_dim(solution, clamped, 0, keepdims=False)[:, later_cols:]
                )
            blocks = jnp.stack(picks)
            selected = jnp.stack(chosen_rows)
            partial_value = contract(selected, lax.all_gather(blocks, "col", axis=2, tiled=True))
            summed = lax.psum(partial_value, "row")
        split_at = summed.shape[1] - rhs_width
        remaining = jnp.concatenate(
            [-summed[:, :split_at], gathered[current_sup] - summed[:, split_at:]], axis=1
        )
        right = jnp.concatenate([unit_block, remaining], axis=1)
        fresh = jnp.dot(
            lower_inv[current_sup].T, right, precision=HIGHEST, preferred_element_type=jnp.float32
        )
        solution = solution.at[current_sup, :, current_sup * col_width :].set(fresh)
    mean_x = solution[:, :, super_count * col_width :]
    unit_part = solution[:, :, : super_count * col_width]
    squares = jnp.sum(unit_part * unit_part, axis=2)
    variance = lax.psum(squares, "col")
    return (mean_x, variance)


def solution(mesh):
    return jax.shard_map(
        body,
        mesh=mesh,
        in_specs=(
            P(None, "row", None, "col"),
            P(None, None, "row"),
            P(None, None, "row"),
            P(),
            P(None, "row", "col"),
        ),
        out_specs=(P(None, "row", "col"), P(None, "row")),
        check_vma=False,
    )
```

profile of v0, /device:TPU:0, one launch (start us, length us, event | category | flops | bytes accessed | tf_op | source)
XLA Modules:
  0.0 1485.7 jit_solution(14807575500122001028)
XLA Ops:
  15.8 15.3 %broadcast_multiply_fusion = f32[6,512,6,256]{3,1,2,0:T(8,128)} fusion(f32[6,512,6,256]{3,1,2,0:T(8,128)} %param.17, f32[6,512,6]{1,2,0:T(8,128)S(1)} %multiply_bitcast_fusion.10), kind=kLoop, calls=%fused_computation.18 | loop fusion | flops 4718592 | bytes 37822464 | tf_op jit(solution)/shard_map/mul | solution.py:38
  31.1 10.7 fusion.93
  43.1 8.5 all_gather.18
  53.4 10.7 broadcast_select_fusion
  64.1 8.5 copy-done
  72.5 3.9 fusion.76
  78.6 92.2 %all-gather.6.cloned.1.call-done = f32[2,512,2048]{2,1,0:T(8,128)} async-done(((f32[2,512,256]{2,1,0:T(8,128)}), f32[2,512,2048]{2,1,0:T(8,128)}) %all-gather.6.cloned.1.call-update) | async-done | bytes 8388624 | tf_op jit(solution)/shard_map/all_gather | solution.py:69
  170.8 11.2 convolution_bitcast_fusion.4
  190.5 9.0 scatter.20
  199.4 33.4 %all-reduce.7.cloned.1.call-done = f32[2048,264]{0,1:T(8,128)} async-done(((f32[2048,264]{0,1:T(8,128)}), f32[2048,264]{0,1:T(8,128)}) %all-reduce.7.cloned.1.call-update) | async-done | bytes 2162704 | tf_op jit(solution)/shard_map/psum | solution.py:70
  235.5 9.8 fusion.73
  245.3 3.7 dynamic-slice_bitcast_fusion.7
  251.2 108.7 %all-gather.8.cloned.1.call-done = f32[2,512,2048]{2,1,0:T(8,128)} async-done(((f32[2,512,256]{2,1,0:T(8,128)}), f32[2,512,2048]{2,1,0:T(8,128)}) %all-gather.8.cloned.1.call-update) | async-done | bytes 8388624 | tf_op jit(solution)/shard_map/all_gather | solution.py:69
  359.9 18.0 %convolution_bitcast_fusion.3 = f32[2048,520]{0,1:T(8,128)} fusion(f32[2,512,2048]{2,1,0:T(8,128)} %all-gather.8.cloned.1.call-done, f32[1,512,520]{1,2,0:T(8,128)} %slice_bitcast_fusion.38, f32[1,512,520]{1,2,0:T(8,128)} %slice_bitcast_fusion.39), kind=kOutput, calls=%fused_computation.57 | convolution fusion | flops 13086760960 | bytes 14778368 | tf_op jit(solution)/shard_map/tiw,tin->wn/dot_general | solution.py:13
  380.1 82.8 %all-reduce.9.cloned.1.call-done = f32[2048,520]{0,1:T(8,128)} async-done(((f32[2048,520]{0,1:T(8,128)}), f32[2048,520]{0,1:T(8,128)}) %all-reduce.9.cloned.1.call-update) | async-done | bytes 4259856 | tf_op jit(solution)/shard_map/psum | solution.py:70
  466.3 13.2 bitcast_dynamic-update-slice_fusion
  485.7 104.2 %all-gather.10.cloned.1.call-done = f32[2,512,2048]{2,1,0:T(8,128)} async-done(((f32[2,512,256]{2,1,0:T(8,128)}), f32[2,512,2048]{2,1,0:T(8,128)}) %all-gather.10.cloned.1.call-update) | async-done | bytes 8388624 | tf_op jit(solution)/shard_map/all_gather | solution.py:69
  589.9 25.4 %convolution_bitcast_fusion.2 = f32[2048,776]{0,1:T(8,128)} fusion(f32[2,512,2048]{2,1,0:T(8,128)} %all-gather.10.cloned.1.call-done, f32[1,512,776]{1,2,0:T(8,128)} %slice_bitcast_fusion.28, f32[1,512,776]{1,2,0:T(8,128)} %slice_bitcast_fusion.29), kind=kOutput, calls=%fused_computation.56 | convolution fusion | flops 19529474048 | bytes 17924096 | tf_op jit(solution)/shard_map/tiw,tin->wn/dot_general | solution.py:13
  623.3 111.1 %all-reduce.11.cloned.1.call-done = f32[2048,776]{0,1:T(8,128)} async-done(((f32[2048,776]{0,1:T(8,128)}), f32[2048,776]{0,1:T(8,128)}) %all-reduce.11.cloned.1.call-update) | async-done | bytes 6357008 | tf_op jit(solution)/shard_map/psum | solution.py:70
  738.6 17.0 %fusion.53 = f32[6,512,1544]{1,2,0:T(8,128)} fusion(f32[6,512,1544]{1,2,0:T(8,128)} %bitcast_dynamic-update-slice_fusion, f32[2048,8]{0,1:T(8,128)S(1)} %slice_subtract_fusion.2, f32[2048,768]{0,1:T(8,128)S(1)} %slice_negate_fusion.2, f32[2048,256]{0,1:T(8,128)S(1)} %fusion.67, f32[6,2048,512]{2,1,0:T(8,128)} %copy-done), kind=kOutput, calls=%fused_computation.63 | convolution fusion | flops 12989792256 | bytes 14761984 | tf_op jit(solution)/shard_map/dot_general | solution.py:76
  762.1 99.4 %all-gather.12.cloned.1.call-done = f32[2,512,2048]{2,1,0:T(8,128)} async-done(((f32[2,512,256]{2,1,0:T(8,128)}), f32[2,512,2048]{2,1,0:T(8,128)}) %all-gather.12.cloned.1.call-update) | async-done | bytes 8388624 | tf_op jit(solution)/shard_map/all_gather | solution.py:69
  861.5 31.5 %convolution_bitcast_fusion.1 = f32[2048,1032]{0,1:T(8,128)} fusion(f32[2,512,2048]{2,1,0:T(8,128)} %all-gather.12.cloned.1.call-done, f32[1,512,1032]{1,2,0:T(8,128)} %slice_bitcast_fusion.26, f32[1,512,1032]{1,2,0:T(8,128)} %slice_bitcast_fusion.27), kind=kOutput, calls=%fused_computation.20 | convolution fusion | flops 25972187136 | bytes 21069824 | tf_op jit(solution)/shard_map/tiw,tin->wn/dot_general | solution.py:13
  894.4 150.9 %all-reduce.13.cloned.1.call-done = f32[2048,1032]{0,1:T(8,128)} async-done(((f32[2048,1032]{0,1:T(8,128)}), f32[2048,1032]{0,1:T(8,128)}) %all-reduce.13.cloned.1.call-update) | async-done | bytes 8454160 | tf_op jit(solution)/shard_map/psum | solution.py:70
  1046.2 4.3 slice_negate_fusion.1
  1050.4 20.4 %fusion.41 = f32[6,512,1544]{1,2,0:T(8,128)} fusion(f32[6,512,1544]{1,2,0:T(8,128)} %fusion.53, f32[2048,8]{0,1:T(8,128)S(1)} %slice_subtract_fusion.1, f32[2048,1024]{0,1:T(8,128)S(1)} %slice_negate_fusion.1, f32[2048,256]{0,1:T(8,128)S(1)} %fusion.67, f32[6,2048,512]{2,1,0:T(8,128)} %copy-done), kind=kOutput, calls=%fused_computation.59 | convolution fusion | flops 16212066304 | bytes 17383424 | tf_op jit(solution)/shard_map/dot_general | solution.py:76
  1077.9 94.5 %all-gather.14.cloned.1.call-done = f32[2,512,2048]{2,1,0:T(8,128)} async-done(((f32[2,512,256]{2,1,0:T(8,128)}), f32[2,512,2048]{2,1,0:T(8,128)}) %all-gather.14.cloned.1.call-update) | async-done | bytes 8388624 | tf_op jit(solution)/shard_map/all_gather | solution.py:69
  1172.5 42.1 %convolution_bitcast_fusion = f32[2048,1288]{0,1:T(8,128)} fusion(f32[2,512,2048]{2,1,0:T(8,128)} %all-gather.14.cloned.1.call-done, f32[1,512,1288]{1,2,0:T(8,128)} %slice_bitcast_fusion.24, f32[1,512,1288]{1,2,0:T(8,128)} %slice_bitcast_fusion.25), kind=kOutput, calls=%fused_computation.19 | convolution fusion | flops 32414900224 | bytes 24215552 | tf_op jit(solution)/shard_map/tiw,tin->wn/dot_general | solution.py:13
  1214.6 186.2 %all-reduce.15.cloned.1.call-done = f32[2048,1288]{0,1:T(8,128)} async-done(((f32[2048,1288]{0,1:T(8,128)}), f32[2048,1288]{0,1:T(8,128)}) %all-reduce.15.cloned.1.call-update) | async-done | bytes 10551312 | tf_op jit(solution)/shard_map/psum | solution.py:70
  1400.7 5.1 slice_negate_fusion
  1406.7 23.9 %fusion.47 = f32[6,512,1544]{1,2,0:T(8,128)} fusion(f32[6,512,1544]{1,2,0:T(8,128)} %fusion.41, f32[2048,8]{0,1:T(8,128)S(1)} %slice_subtract_fusion, f32[2048,1280]{0,1:T(8,128)S(1)} %slice_negate_fusion, f32[2048,256]{0,1:T(8,128)S(1)} %fusion.67, f32[6,2048,512]{2,1,0:T(8,128)} %copy-done), kind=kOutput, calls=%fused_computation.61 | convolution fusion | flops 19434340352 | bytes 20004864 | tf_op jit(solution)/shard_map/dot_general | solution.py:76
  1432.1 8.8 fusion
  1440.9 37.7 %psum.47 = f32[6,512]{1,0:T(8,128)} all-reduce(f32[6,512]{1,0:T(8,128)S(1)} %fusion), channel_id=1, replica_groups=mesh['row'=4,'col'=8] {'col'}, use_global_device_ids=true, to_apply=%region_10.11 | all-reduce | flops 3072 | bytes 24576 | tf_op jit(solution)/shard_map/psum | solution.py:83
  (77 shorter events, 56.6 us)
Async XLA Ops:
  7.2 163.6 %all-gather.6.cloned.1.call-start = ((), (), s32[]{:S(2)}) async-start(), calls=%async_computation | async-start | bytes 9437184 | tf_op jit(solution)/shard_map/all_gather | solution.py:69
  41.8 1.3 copy-start.4
  43.0 189.8 %all-reduce.7.cloned.1.call-start = ((), (), s32[]{:S(2)}) async-start(), calls=%async_computation.1 | async-start | bytes 4325376 | tf_op jit(solution)/shard_map/psum | solution.py:70
  51.6 0.8 copy-start.2
  64.1 8.5 copy-start
  182.0 177.9 %all-gather.8.cloned.1.call-start = ((), (), s32[]{:S(2)}) async-start(), calls=%async_computation.2 | async-start | bytes 9437184 | tf_op jit(solution)/shard_map/all_gather | solution.py:69
  190.4 42.4 %copy-start.3 = (f32[6,2048,8]{1,2,0:T(8,128)S(1)}, f32[6,2048,8]{1,2,0:T(8,128)}, u32[]{:S(2)}) copy-start(f32[6,2048,8]{1,2,0:T(8,128)} %copy-done.2) | copy-start | bytes 1179652
  190.4 272.5 %all-reduce.9.cloned.1.call-start = ((), (), s32[]{:S(2)}) async-start(), calls=%async_computation.3 | async-start | bytes 8519680 | tf_op jit(solution)/shard_map/psum | solution.py:70
  378.0 1.0 copy-start.1
  378.0 211.9 %all-gather.10.cloned.1.call-start = ((), (), s32[]{:S(2)}) async-start(), calls=%async_computation.4 | async-start | bytes 9437184 | tf_op jit(solution)/shard_map/all_gather | solution.py:69
  380.0 354.3 %all-reduce.11.cloned.1.call-start = ((), (), s32[]{:S(2)}) async-start(), calls=%async_computation.5 | async-start | bytes 12713984 | tf_op jit(solution)/shard_map/psum | solution.py:70
  615.3 246.2 %all-gather.12.cloned.1.call-start = ((), (), s32[]{:S(2)}) async-start(), calls=%async_computation.6 | async-start | bytes 9437184 | tf_op jit(solution)/shard_map/all_gather | solution.py:69
  623.2 422.1 %all-reduce.13.cloned.1.call-start = ((), (), s32[]{:S(2)}) async-start(), calls=%async_computation.7 | async-start | bytes 16908288 | tf_op jit(solution)/shard_map/psum | solution.py:70
  893.0 279.4 %all-gather.14.cloned.1.call-start = ((), (), s32[]{:S(2)}) async-start(), calls=%async_computation.8 | async-start | bytes 9437184 | tf_op jit(solution)/shard_map/all_gather | solution.py:69
  894.2 506.6 %all-reduce.15.cloned.1.call-start = ((), (), s32[]{:S(2)}) async-start(), calls=%async_computation.9 | async-start | bytes 21102592 | tf_op jit(solution)/shard_map/psum | solution.py:70
Sparse Core Ops, SparseCore 0:
  43.1 127.6 all-gather.5
  182.1 50.6 all-reduce.6
  234.9 124.9 all-gather.7
  378.1 84.7 all-reduce.8
  464.8 125.0 all-gather.9
  615.5 118.8 all-reduce.10
  736.4 125.1 all-gather.11
  893.2 152.0 all-reduce.12
  1047.4 125.0 all-gather.13
  1214.7 185.9 all-reduce.14
where the time goes:
time: 1490 us
  waiting for transfers between devices  1060 us (71%)
  matrix products  216 us (14%)
  other arithmetic  70.2 us (5%)
  local copies, waits for them, and re-layouts  61.6 us (4%)
  blocking collectives  46.2 us (3%)
  between operations  27.1 us (2%)
    psum x5, waiting for transfers between devices, body(): summed = lax.psum(partial_value, 'row')  564 us
    all_gather x5, waiting for transfers between devices, body(): lax.all_gather(blocks, 'col', axis=2, tiled=True)  499 us
    dot_general x5, matrix products, contract(): return jnp.einsum('tiw,tin->wn', panel_piece, selected, precision=HIGHEST)  128 us
    dot_general x6, matrix products, body(): jnp.dot(lower_inv[current_sup].T, right, precision=HIGHEST, preferred_ele...  88.2 us
    psum x1, blocking collectives, body(): variance = lax.psum(squares, 'col')  37.7 us
  transfers between devices with their start and end apart: 10, of which 10 were waited for; matrix products, arithmetic and copies ran while one was open for 9% of the time, Pallas kernels for 0%

commit v1 on v0

v1 whole, which is shorter than its diff:
```python
import jax
import jax.numpy as jnp
from jax import lax
from jax.sharding import PartitionSpec as P

HIGH = lax.Precision.HIGH


def product(left, right):
    return jnp.dot(left, right, precision=HIGH, preferred_element_type=jnp.float32)


def body(factor, diag_inv, structure, parent, post):
    super_count = factor.shape[0]
    row_width = factor.shape[1]
    col_width = factor.shape[3]
    full_width = diag_inv.shape[1]
    row_at = lax.axis_index("row")
    col_at = lax.axis_index("col")
    last = super_count - 1
    block_rows = row_width // structure.shape[2]

    extended = jnp.concatenate([parent, jnp.full((1,), super_count, jnp.int32)])
    first_at = parent
    second_at = extended[parent]

    def pick(current_sup, target):
        clamped = jnp.minimum(target, last)
        block = lax.dynamic_index_in_dim(factor[:, :, current_sup, :], clamped, 0, keepdims=False)
        flags = lax.dynamic_index_in_dim(structure[current_sup], clamped, 0, keepdims=False)
        flags = jnp.where(target < super_count, flags.astype(jnp.float32), 0.0)
        return block * jnp.repeat(flags, block_rows)[:, None]

    blocks = [None] * super_count
    for current_sup in range(last - 1, -1, -1):
        mine = jnp.concatenate(
            [pick(current_sup, first_at[current_sup]), pick(current_sup, second_at[current_sup])], axis=0
        )
        blocks[current_sup] = lax.all_gather(mine, "col", axis=1, tiled=True)

    own_cols = row_at * row_width + jnp.arange(row_width, dtype=jnp.int32)
    rows_full = jnp.arange(full_width, dtype=jnp.int32)
    keep = rows_full[:, None] >= own_cols[None, :]
    lower = [jnp.where(keep, diag_inv[s], 0.0) for s in range(super_count)]
    unit_rows = col_at * col_width + jnp.arange(col_width, dtype=jnp.int32)
    own = lax.dynamic_slice_in_dim(diag_inv, col_at * col_width, col_width, axis=1)
    own = jnp.where((unit_rows[:, None] >= own_cols[None, :])[None], own, 0.0)
    gathered = jnp.swapaxes(lax.all_gather(post, "row", axis=1, tiled=True), 1, 2)

    def take(stacked, target):
        return lax.dynamic_index_in_dim(stacked, jnp.minimum(target, last), 0, keepdims=False)

    rhs = jnp.stack([product(gathered[s], lower[s]) for s in range(super_count)])

    def solve(current_sup, unit_part, rhs_part):
        summed = lax.psum(jnp.concatenate([unit_part, rhs_part], axis=0), "row")
        right = jnp.concatenate(
            [-summed[:col_width], gathered[current_sup] - summed[col_width:]], axis=0
        )
        fresh = product(right, lower[current_sup])
        return fresh[:col_width], fresh[col_width:]

    near = [jnp.zeros((col_width, row_width), jnp.float32)] * super_count
    means = [rhs[s] for s in range(super_count)]
    for s in range(last - 1, -1, -1):
        one, two = first_at[s], second_at[s]
        unit_part = product(take(own, one), blocks[s][:row_width])
        rhs_part = product(
            jnp.concatenate([take(rhs, one), take(rhs, two)], axis=1), blocks[s]
        )
        near[s], means[s] = solve(s, unit_part, rhs_part)
    near_all = jnp.stack(near)
    rhs = jnp.stack(means)

    far = [None] * super_count
    for s in range(last - 1, -1, -1):
        one, two = first_at[s], second_at[s]
        selected = jnp.concatenate(
            [
                jnp.concatenate([take(near_all, one), take(own, two)], axis=1),
                jnp.concatenate([take(rhs, one), take(rhs, two)], axis=1),
            ],
            axis=0,
        )
        both = product(selected, blocks[s])
        far[s], means[s] = solve(s, both[:col_width], both[col_width:])

    squares = []
    for s in range(super_count):
        total = jnp.sum(own[s] * own[s], axis=0)
        if s < last:
            total = total + jnp.sum(near[s] * near[s], axis=0) + jnp.sum(far[s] * far[s], axis=0)
        squares.append(total)
    variance = lax.psum(jnp.stack(squares), "col")
    mean_x = jnp.swapaxes(jnp.stack(means), 1, 2)
    return (mean_x, variance)


def solution(mesh):
    return jax.shard_map(
        body,
        mesh=mesh,
        in_specs=(
            P(None, "row", None, "col"),
            P(None, None, "row"),
            P(None, None, "row"),
            P(),
            P(None, "row", "col"),
        ),
        out_specs=(P(None, "row", "col"), P(None, "row")),
        check_vma=False,
    )
```

time: 1490 us -> 1190 us (0.80)
  waiting for transfers between devices: 1060 us -> 910 us
  matrix products: 216 us -> 144 us
  local copies, waits for them, and re-layouts: 61.6 us -> 24.2 us
  other arithmetic: 70.2 us -> 36.7 us
    psum x5 -> x2, waiting for transfers between devices: 564 us -> 380 us  [solve(): summed = lax.psum(jnp.concatenate([unit_part, rhs_part], axis=0), 'row')]
    dot_general x11 -> x31, matrix products: 216 us -> 144 us  [product(): jnp.dot(left, right, precision=HIGH, preferred_element_type=jnp.float32)]
    all_gather x5, waiting for transfers between devices: 499 us -> 530 us  [body(): blocks[current_sup] = lax.all_gather(mine, 'col', axis=1, tiled=True)]
    concatenate x0 -> x10, other arithmetic: none -> 15.3 us  [the longest x5 7.7 us: body(): jnp.concatenate([pick(current_sup, first_at[current_sup]), pick(current_s...]
  transfers between devices with their start and end apart: 10 -> 7, of which waited for: 10 -> 7; matrix products, arithmetic and copies ran while one was open for 9% -> 7% of each run, Pallas kernels for 0% -> 0%
where the time goes in v1:
time: 1190 us
  waiting for transfers between devices  910 us (76%)
  matrix products  144 us (12%)
  blocking collectives  46.6 us (4%)
  other arithmetic  36.7 us (3%)
  between operations  27.8 us (2%)
  local copies, waits for them, and re-layouts  24.2 us (2%)
    all_gather x5, waiting for transfers between devices, body(): blocks[current_sup] = lax.all_gather(mine, 'col', axis=1, tiled=True)  530 us
    psum x2, waiting for transfers between devices, solve(): summed = lax.psum(jnp.concatenate([unit_part, rhs_part], axis=0), 'row')  380 us
    dot_general x31, matrix products, product(): jnp.dot(left, right, precision=HIGH, preferred_element_type=jnp.float32)  144 us
    psum x1, blocking collectives, body(): variance = lax.psum(jnp.stack(squares), 'col')  37.7 us
  transfers between devices with their start and end apart: 7, of which 7 were waited for; matrix products, arithmetic and copies ran while one was open for 7% of the time, Pallas kernels for 0%

profile of v1, /device:TPU:0, one launch (start us, length us, event | category | flops | bytes accessed | tf_op | source)
XLA Modules:
  0.0 1189.7 jit_solution(15968273963925713293)
XLA Ops:
  17.9 11.0 fusion.291
  51.5 8.9 all_gather.19
  84.9 75.8 %all-gather.8.cloned.1.call-done = f32[1024,2048]{1,0:T(8,128)} async-done(((f32[1024,256]{1,0:T(8,128)}), f32[1024,2048]{1,0:T(8,128)}) %all-gather.8.cloned.1.call-update) | async-done | bytes 8388624 | tf_op jit(solution)/shard_map/all_gather | solution.py:39
  160.8 4.2 fusion.6
  165.0 5.9 fusion.204
  172.4 113.5 %all-gather.10.cloned.1.call-done = f32[1024,2048]{1,0:T(8,128)} async-done(((f32[1024,256]{1,0:T(8,128)}), f32[1024,2048]{1,0:T(8,128)}) %all-gather.10.cloned.1.call-update) | async-done | bytes 8388624 | tf_op jit(solution)/shard_map/all_gather | solution.py:39
  290.2 5.7 fusion.208
  297.4 113.8 %all-gather.12.cloned.1.call-done = f32[1024,2048]{1,0:T(8,128)} async-done(((f32[1024,256]{1,0:T(8,128)}), f32[1024,2048]{1,0:T(8,128)}) %all-gather.12.cloned.1.call-update) | async-done | bytes 8388624 | tf_op jit(solution)/shard_map/all_gather | solution.py:39
  411.2 4.2 fusion.2
  415.4 5.7 fusion.212
  422.6 113.6 %all-gather.14.cloned.1.call-done = f32[1024,2048]{1,0:T(8,128)} async-done(((f32[1024,256]{1,0:T(8,128)}), f32[1024,2048]{1,0:T(8,128)}) %all-gather.14.cloned.1.call-update) | async-done | bytes 8388624 | tf_op jit(solution)/shard_map/all_gather | solution.py:39
  540.4 6.1 fusion.216
  548.1 113.2 %all-gather.6.cloned.1.call-done = f32[1024,2048]{1,0:T(8,128)} async-done(((f32[1024,256]{1,0:T(8,128)}), f32[1024,2048]{1,0:T(8,128)}) %all-gather.6.cloned.1.call-update) | async-done | bytes 8388624 | tf_op jit(solution)/shard_map/all_gather | solution.py:39
  665.5 5.5 fusion.200
  675.0 188.1 %all-reduce.7.cloned.1.call-done = (f32[264,2048]{1,0:T(8,128)}, f32[264,2048]{1,0:T(8,128)}, f32[264,2048]{1,0:T(8,128)}, f32[264,2048]{1,0:T(8,128)}, f32[264,2048]{1,0:T(8,128)}) async-done(((f32[264,2048]{1,0:T(8,128)}, f32[264,2048]{1,0:T(8,128)}, f32[264,2048]{1,0:T(8,128)}, f32[264,2048]{1,0:T(8,128)}, f32[264,2048]{1,0:T(8,128)}), (f32[264,2048]{1,0:T(8,128)}, f32[264,2048]{1,0:T(8,128)}, ...) | async-done | bytes 10813456 | tf_op jit(solution)/shard_map/psum | solution.py:56
  869.9 4.2 fusion.35
  874.1 4.3 fusion.37
  878.4 4.3 fusion.39
  882.7 4.3 fusion.41
  887.0 4.4 fusion.43
  893.8 6.0 fusion.139
  899.9 5.8 fusion.147
  905.8 5.8 fusion.155
  911.6 6.1 fusion.163
  917.7 5.8 fusion.171
  923.9 192.1 %all-reduce.5.cloned.1.call-done = (f32[264,2048]{1,0:T(8,128)}, f32[264,2048]{1,0:T(8,128)}, f32[264,2048]{1,0:T(8,128)}, f32[264,2048]{1,0:T(8,128)}, f32[264,2048]{1,0:T(8,128)}) async-done(((f32[264,2048]{1,0:T(8,128)}, f32[264,2048]{1,0:T(8,128)}, f32[264,2048]{1,0:T(8,128)}, f32[264,2048]{1,0:T(8,128)}, f32[264,2048]{1,0:T(8,128)}), (f32[264,2048]{1,0:T(8,128)}, f32[264,2048]{1,0:T(8,128)}, ...) | async-done | bytes 10813456 | tf_op jit(solution)/shard_map/psum | solution.py:56
  1122.6 4.3 fusion.34
  1127.0 4.5 fusion.42
  1131.6 4.3 fusion.40
  1135.9 4.3 fusion.38
  1140.3 4.3 fusion.36
  1144.9 37.7 %psum.87 = f32[6,512]{1,0:T(8,128)} all-reduce(f32[6,512]{1,0:T(8,128)S(1)} %stack.112), channel_id=1, replica_groups=mesh['row'=4,'col'=8] {'col'}, use_global_device_ids=true, to_apply=%region_26.27 | all-reduce | flops 3072 | bytes 24576 | tf_op jit(solution)/shard_map/psum | solution.py:94
  (200 shorter events, 84.2 us)
Async XLA Ops:
  7.2 153.6 %all-gather.8.cloned.1.call-start = ((), (), s32[]{:S(2)}) async-start(), calls=%async_computation.1 | async-start | bytes 9437184 | tf_op jit(solution)/shard_map/all_gather | solution.py:39
  32.8 253.2 %all-gather.10.cloned.1.call-start = ((), (), s32[]{:S(2)}) async-start(), calls=%async_computation.2 | async-start | bytes 9437184 | tf_op jit(solution)/shard_map/all_gather | solution.py:39
  35.1 376.1 %all-gather.12.cloned.1.call-start = ((), (), s32[]{:S(2)}) async-start(), calls=%async_computation.3 | async-start | bytes 9437184 | tf_op jit(solution)/shard_map/all_gather | solution.py:39
  45.1 491.1 %all-gather.14.cloned.1.call-start = ((), (), s32[]{:S(2)}) async-start(), calls=%async_computation.4 | async-start | bytes 9437184 | tf_op jit(solution)/shard_map/all_gather | solution.py:39
  47.5 613.8 %all-gather.6.cloned.1.call-start = ((), (), s32[]{:S(2)}) async-start(), calls=%async_computation | async-start | bytes 9437184 | tf_op jit(solution)/shard_map/all_gather | solution.py:39
  51.4 811.7 %all-reduce.7.cloned.1.call-start = ((), (), s32[]{:S(2)}) async-start(), calls=%async_computation.6 | async-start | bytes 21626880 | tf_op jit(solution)/shard_map/psum | solution.py:56
  51.5 30.9 %copy-start.13 = (s32[512]{0:T(512)}, s32[512]{0:T(512)S(1)}, u32[]{:S(2)}) copy-start(s32[512]{0:T(512)S(1)} %iota_add_fusion) | copy-start | bytes 6148
  160.8 4.2 copy-start.24
  286.0 4.2 copy-start.22
  411.2 4.2 copy-start.20
  536.2 4.2 copy-start.18
  672.6 443.4 %all-reduce.5.cloned.1.call-start = ((), (), s32[]{:S(2)}) async-start(), calls=%async_computation.5 | async-start | bytes 21626880 | tf_op jit(solution)/shard_map/psum | solution.py:56
  887.0 5.0 slice-start.8
  891.7 8.1 slice-start
  893.8 6.0 slice-start.1
  893.8 6.0 copy-start.11
  893.8 11.9 slice-start.2
  899.8 5.9 slice-start.3
  899.9 5.9 copy-start.10
  899.9 11.7 slice-start.4
  905.7 5.9 slice-start.5
  905.7 5.9 copy-start.9
  905.8 11.9 %slice-start.6 = ((s8[8388608]{0:T(1024)(128)(4,1)}), s8[4194304]{0:T(1024)(128)(4,1)S(1)}, s32[]{:S(2)}) async-start(s8[8388608]{0:T(1024)(128)(4,1)} %bitcast.345), calls=%async_computation.13 | async-start | bytes 8388608
  911.6 6.1 slice-start.7
  911.6 6.1 copy-start.8
  1140.3 4.5 copy-start.30
  1140.3 4.5 copy-start.29
  1140.3 4.5 copy-start.28
  1140.3 4.5 copy-start.27
  1140.3 4.5 copy-start.26
  1140.3 4.5 copy-start.25
  1144.7 37.8 %copy-start.31 = (f32[6,8,512]{2,1,0:T(8,128)}, f32[6,8,512]{2,1,0:T(8,128)S(1)}, u32[]{:S(2)}) copy-start(f32[6,8,512]{2,1,0:T(8,128)S(1)} %constant_dynamic-update-slice_fusion.7) | copy-start | bytes 294916
  (17 other events, 46.8 us)
Sparse Core Ops, SparseCore 0:
  32.9 127.8 all-gather.7
  162.8 123.1 all-gather.9
  288.0 123.1 all-gather.11
  413.1 123.1 all-gather.13
  538.1 123.1 all-gather.5
  672.7 190.3 all-reduce.6
  923.7 192.3 all-reduce.4
